TPU v7x, 32 devices: a whole 2x2x4 slice. The times are simulated.
32 devices in a mesh: val: 2 (over x), pts: 16 (over z, y, core).
Axes of the slice: x: 2, y: 2, z: 4, core: 2. Of those that a mesh axis runs over, the one named last changes fastest.
Arguments:
- trial: bfloat16 [512, 16384], P('val', 'pts'), may hold values from -6 to 6
- energy_gap: float32 [512, 512], P('val', 'pts'), may hold values from 0.5 to 3.5
- orb_val: bfloat16 [512, 16384], P('val'), may hold values from -0.25 to 0.25
- orb_cond: bfloat16 [512, 16384], P('pts'), may hold values from -0.25 to 0.25
- kernel: bfloat16 [16384, 16384], P('pts', 'val'), may hold values from -0.046875 to 0.046875
Outputs:
- first_step: bfloat16 [512, 16384], P('val', 'pts')
- filtered: bfloat16 [512, 16384], P('val', 'pts')
All inputs are finite; a program needn't handle non-finite values.
Results may differ from a plain program's by a relative error of at most 0.029.
Values may be sent and summed in bfloat16 or wider, within the bound.
A program may use at most 128 MiB of HBM per device.

v0:
```python
import math

import jax
import jax.numpy as jnp
from jax import lax
from jax.sharding import PartitionSpec as P

K = 32


CENTER = 2.0
HALF_WIDTH = 1.5


def pair_cols(val_block, cond_block, val_first, cond_first, width):
    val_cols = lax.dynamic_slice_in_dim(val_block, val_first, width, 1).astype(jnp.float32)
    cond_cols = lax.dynamic_slice_in_dim(cond_block, cond_first, width, 1).astype(jnp.float32)
    table = val_cols[:, None, :] * cond_cols[None, :, :]
    return table.reshape(val_block.shape[0] * cond_block.shape[0], width).astype(jnp.bfloat16)


def pair_block(orb_val, orb_cond, first_col, width):
    return pair_cols(orb_val, orb_cond, first_col, first_col, width)


def coupling(trial_loc, orb_val, val_columns, orb_cond, kernel):
    val_count = trial_loc.shape[0]
    cond_count = orb_cond.shape[0]
    col_width = kernel.shape[1]
    whole_trial = lax.all_gather(trial_loc, "val", axis=0, tiled=True)
    all_rows = whole_trial.reshape(whole_trial.shape[0] * cond_count, K)
    col_base = lax.axis_index("val") * col_width
    local_len = math.gcd(col_width, 512)
    local_count = col_width // local_len

    def local_block(number):
        offset = number * local_len
        pairs = pair_cols(val_columns, orb_cond, offset, col_base + offset, local_len)
        return lax.dot_general(
            pairs, all_rows, (((0,), (0,)), ((), ())), preferred_element_type=jnp.float32
        )

    local_fit = lax.map(local_block, jnp.arange(local_count, dtype=jnp.int32)).reshape(col_width, K)
    summed = lax.psum(local_fit.astype(jnp.bfloat16), "pts").astype(jnp.float32)
    fit_coefs = summed.T.astype(jnp.bfloat16)
    kernel_part = lax.dot_general(
        fit_coefs, kernel, (((1,), (1,)), ((), ())), preferred_element_type=jnp.float32
    )
    kernel_out = lax.psum(kernel_part.astype(jnp.bfloat16), "val")
    initial = jnp.zeros((val_count * cond_count, K), jnp.float32)
    field_piece = lax.all_gather(kernel_out, "pts", axis=1, tiled=True)
    piece_len = field_piece.shape[1]
    block_len = math.gcd(piece_len, 512)
    block_count = piece_len // block_len

    def decode_block(number, running):
        offset = number * block_len
        pairs = pair_block(orb_val, orb_cond, offset, block_len)
        coef_block = lax.dynamic_slice_in_dim(field_piece, offset, block_len, 1)
        added = lax.dot_general(
            pairs, coef_block, (((1,), (1,)), ((), ())), preferred_element_type=jnp.float32
        )
        return running + added

    decoded = lax.fori_loop(0, block_count, decode_block, initial)
    return decoded.reshape(val_count, cond_count, K)


def filter_apply(trial_loc, energy_gap, orb_val, val_columns, orb_cond, kernel):
    val_count = trial_loc.shape[0]
    cond_count = orb_cond.shape[0]
    current = trial_loc.astype(jnp.float32).reshape(val_count, cond_count, K)
    coupled = coupling(trial_loc, orb_val, val_columns, orb_cond, kernel)
    return (energy_gap[:, :, None] * current + 2.0 * coupled - CENTER * current) / HALF_WIDTH


def on_device(trial, energy_gap, orb_val, orb_cond, kernel):
    val_count = trial.shape[0]
    cond_count = orb_cond.shape[0]
    val_columns = lax.all_to_all(orb_val, "val", split_axis=1, concat_axis=0, tiled=True)
    first_step = filter_apply(trial, energy_gap, orb_val, val_columns, orb_cond, kernel)
    first_step = first_step.reshape(val_count, cond_count * K).astype(jnp.bfloat16)
    second = 2.0 * filter_apply(first_step, energy_gap, orb_val, val_columns, orb_cond, kernel)
    second = second - trial.astype(jnp.float32).reshape(val_count, cond_count, K)
    return (first_step, second.reshape(val_count, cond_count * K).astype(jnp.bfloat16))


def solution(mesh):
    placed = (P("val", "pts"), P("val", "pts"), P("val", None), P("pts", None), P("pts", "val"))
    return jax.shard_map(
        on_device,
        mesh=mesh,
        in_specs=placed,
        out_specs=(P("val", "pts"), P("val", "pts")),
        check_vma=False,
    )
```

profile of v0, /device:TPU:0, one launch (start us, length us, event | category | flops | bytes accessed | tf_op | source)
XLA Modules:
  0.0 1795.1 jit_solution(6012039507727609798)
XLA Ops:
  7.2 7.6 copy.26
  14.8 6.9 all-to-all-start
  22.5 37.4 %all-gather.5.cloned.1.call-done = bf16[512,1024]{1,0:T(8,128)(2,1)} async-done(((bf16[256,1024]{1,0:T(8,128)(2,1)}), bf16[512,1024]{1,0:T(8,128)(2,1)}) %all-gather.5.cloned.1.call-update) | async-done | bytes 1048592 | tf_op jit(solution)/shard_map/all_gather | solution.py:30
  66.1 60.7 %all-to-all-done = bf16[256,2,8192]{2,0,1:T(8,128)(2,1)} async-done(((bf16[256,2,8192]{2,0,1:T(8,128)(2,1)}), bf16[256,2,8192]{2,0,1:T(8,128)(2,1)}, u32[]{:S(2)}, u32[]{:S(2)}) %all-to-all-start) | async-done | bytes 8388640 | tf_op jit(solution)/shard_map/all_to_all | solution.py:80
  126.9 178.1 %while.48 = (s32[]{:T(128)}, bf16[16,512,32]{1,2,0:T(8,128)(2,1)S(1)}, s32[16]{0:T(128)S(1)}, bf16[512,8192]{1,0:T(8,128)(2,1)}, s32[]{:T(128)}, /*index=5*/bf16...) while((s32[]{:T(128)}, ...), condition=%wide.region_1.2_spmd, body=%wide.region_0.1_spmd.sunk | while | flops 553926656 | bytes 44794116 | solution.py:43
  305.9 91.3 %all-reduce.5.cloned.1.call-done = bf16[8192,32]{0,1:T(8,128)(2,1)} async-done(((bf16[8192,32]{0,1:T(8,128)(2,1)}), bf16[8192,32]{0,1:T(8,128)(2,1)}) %all-reduce.5.cloned.1.call-update) | async-done | bytes 524304 | tf_op jit(solution)/shard_map/psum | solution.py:44
  397.3 11.6 convolution_convert_fusion.1
  409.0 21.5 %all-reduce.7.cloned.1.call-done = bf16[32,1024]{1,0:T(8,128)(2,1)} async-done(((bf16[32,1024]{1,0:T(8,128)(2,1)}), bf16[32,1024]{1,0:T(8,128)(2,1)}) %all-reduce.7.cloned.1.call-update) | async-done | bytes 65552 | tf_op jit(solution)/shard_map/psum | solution.py:49
  431.0 39.5 %all-gather.7.cloned.1.call-done = bf16[32,16384]{1,0:T(8,128)(2,1)} async-done(((bf16[32,1024]{1,0:T(8,128)(2,1)}), bf16[32,16384]{1,0:T(8,128)(2,1)}) %all-gather.7.cloned.1.call-update) | async-done | bytes 1048592 | tf_op jit(solution)/shard_map/all_gather | solution.py:51
  470.4 461.6 %while.50 = (s32[]{:T(128)}, f32[8192,32]{0,1:T(8,128)S(1)}, bf16[256,16384]{1,0:T(8,128)(2,1)}, bf16[32,16384]{1,0:T(8,128)(2,1)}, bf16[32,16384]{1,0:T(8,128)(...) while((s32[]{:T(128)}, f32[8192,32]{0,1:T(8,128)S(1)}, bf16[256,16384]{1,0:T(8,128)(2,1)}, ...), condition=%wide.region_5.6_spmd.clone, body=%wide.region_4.5_spmd.clone.sunk | while | flops 277495808 | bytes 20381856 | solution.py:65
  944.2 20.3 %all-gather.9.cloned.1.call-done = bf16[512,1024]{0,1:T(8,128)(2,1)} async-done(((bf16[256,1024]{0,1:T(8,128)(2,1)}), bf16[512,1024]{0,1:T(8,128)(2,1)}) %all-gather.9.cloned.1.call-update) | async-done | bytes 1048592 | tf_op jit(solution)/shard_map/all_gather | solution.py:30
  970.5 177.8 %while.49 = (s32[]{:T(128)}, bf16[16,512,32]{1,2,0:T(8,128)(2,1)S(1)}, s32[16]{0:T(128)S(1)}, bf16[512,8192]{1,0:T(8,128)(2,1)}, s32[]{:T(128)}, /*index=5*/bf16...) while((s32[]{:T(128)}, ...), condition=%wide.region_7.8_spmd, body=%wide.region_6.7_spmd.sunk | while | flops 553926656 | bytes 44794116 | solution.py:43
  1149.5 90.6 %all-reduce.9.cloned.1.call-done = bf16[8192,32]{0,1:T(8,128)(2,1)} async-done(((bf16[8192,32]{0,1:T(8,128)(2,1)}), bf16[8192,32]{0,1:T(8,128)(2,1)}) %all-reduce.9.cloned.1.call-update) | async-done | bytes 524304 | tf_op jit(solution)/shard_map/psum | solution.py:44
  1240.1 11.6 convolution_convert_fusion
  1251.8 21.5 %all-reduce.11.cloned.1.call-done = bf16[32,1024]{1,0:T(8,128)(2,1)} async-done(((bf16[32,1024]{1,0:T(8,128)(2,1)}), bf16[32,1024]{1,0:T(8,128)(2,1)}) %all-reduce.11.cloned.1.call-update) | async-done | bytes 65552 | tf_op jit(solution)/shard_map/psum | solution.py:49
  1274.3 39.0 %all-gather.11.cloned.1.call-done = bf16[32,16384]{1,0:T(8,128)(2,1)} async-done(((bf16[32,1024]{1,0:T(8,128)(2,1)}), bf16[32,16384]{1,0:T(8,128)(2,1)}) %all-gather.11.cloned.1.call-update) | async-done | bytes 1048592 | tf_op jit(solution)/shard_map/all_gather | solution.py:51
  1313.4 462.7 %while.51 = (s32[]{:T(128)}, f32[8192,32]{0,1:T(8,128)S(1)}, bf16[256,16384]{1,0:T(8,128)(2,1)}, bf16[32,16384]{1,0:T(8,128)(2,1)}, bf16[32,16384]{1,0:T(8,128)(...) while((s32[]{:T(128)}, f32[8192,32]{0,1:T(8,128)S(1)}, bf16[256,16384]{1,0:T(8,128)(2,1)}, ...), condition=%wide.region_11.12_spmd.clone, body=%wide.region_10.11_spmd.clone.sunk | while | flops 277495808 | bytes 20381856 | solution.py:65
  1315.1 6.7 multiply_convert_fusion.11
  1329.6 6.7 multiply_convert_fusion.11
  1344.1 6.7 multiply_convert_fusion.11
  1358.5 6.7 multiply_convert_fusion.11
  1373.0 6.7 multiply_convert_fusion.11
  1387.4 6.7 multiply_convert_fusion.11
  1401.9 6.7 multiply_convert_fusion.11
  1416.4 6.7 multiply_convert_fusion.11
  1430.8 6.7 multiply_convert_fusion.11
  1445.3 6.7 multiply_convert_fusion.11
  1459.7 6.7 multiply_convert_fusion.11
  1474.2 6.7 multiply_convert_fusion.11
  1488.6 6.7 multiply_convert_fusion.11
  1503.1 6.7 multiply_convert_fusion.11
  1517.6 6.7 multiply_convert_fusion.11
  1532.0 6.7 multiply_convert_fusion.11
  1546.5 6.7 multiply_convert_fusion.11
  1560.9 6.7 multiply_convert_fusion.11
  1575.4 6.7 multiply_convert_fusion.11
  1589.9 6.7 multiply_convert_fusion.11
  1604.3 6.7 multiply_convert_fusion.11
  1618.8 6.7 multiply_convert_fusion.11
  1633.2 6.7 multiply_convert_fusion.11
  1647.7 6.7 multiply_convert_fusion.11
  1662.2 6.7 multiply_convert_fusion.11
  1676.6 6.7 multiply_convert_fusion.11
  1691.1 6.7 multiply_convert_fusion.11
  1705.5 6.7 multiply_convert_fusion.11
  1720.0 6.7 multiply_convert_fusion.11
  1748.9 6.7 multiply_convert_fusion.11
  1763.4 6.7 multiply_convert_fusion.11
  (495 shorter events, 1089.4 us)
Async XLA Ops:
  14.8 112.1 %all-to-all-start = ((bf16[256,2,8192]{2,0,1:T(8,128)(2,1)}), bf16[256,2,8192]{2,0,1:T(8,128)(2,1)}, u32[]{:S(2)}, u32[]{:S(2)}) async-start(bf16[256,2,8192]{2,0,1:T(8,128)(2,1)} %bitcast.82), calls=%async_computation | async-start | bytes 16777216 | tf_op jit(solution)/shard_map/all_to_all | solution.py:80
  21.7 38.2 %all-gather.5.cloned.1.call-start = ((), (), s32[]{:S(2)}) async-start(), calls=%async_computation.1 | async-start | bytes 1572864 | tf_op jit(solution)/shard_map/all_gather | solution.py:30
  22.4 374.8 %all-reduce.5.cloned.1.call-start = ((), (), s32[]{:S(2)}) async-start(), calls=%async_computation.2 | async-start | bytes 1048576 | tf_op jit(solution)/shard_map/psum | solution.py:44
  128.9 6.2 copy-start
  140.1 6.2 copy-start
  151.2 6.2 copy-start
  162.3 6.2 copy-start
  173.5 6.2 copy-start
  184.6 6.2 copy-start
  195.7 6.2 copy-start
  206.8 6.2 copy-start
  218.0 6.2 copy-start
  229.1 6.2 copy-start
  240.2 6.2 copy-start
  251.4 6.2 copy-start
  262.5 6.2 copy-start
  273.6 6.2 copy-start
  284.8 6.2 copy-start
  295.9 6.2 copy-start
  305.0 125.8 %copy-start.3 = (bf16[256,1024]{1,0:T(8,128)(2,1)S(1)}, bf16[256,1024]{1,0:T(8,128)(2,1)}, u32[]{:S(2)}) copy-start(bf16[256,1024]{1,0:T(8,128)(2,1)} %param.13) | copy-start | bytes 1572868
  305.9 124.6 %all-reduce.7.cloned.1.call-start = ((), (), s32[]{:S(2)}) async-start(), calls=%async_computation.3 | async-start | bytes 131072 | tf_op jit(solution)/shard_map/psum | solution.py:49
  408.9 61.5 %all-gather.7.cloned.1.call-start = ((), (), s32[]{:S(2)}) async-start(), calls=%async_computation.4 | async-start | bytes 1114112 | tf_op jit(solution)/shard_map/all_gather | solution.py:51
  430.5 534.0 %all-gather.9.cloned.1.call-start = ((), (), s32[]{:S(2)}) async-start(), calls=%async_computation.5 | async-start | bytes 1572864 | tf_op jit(solution)/shard_map/all_gather | solution.py:30
  470.4 471.5 %copy-start.4 = (f32[256,32]{0,1:T(8,128)S(1)}, f32[256,32]{0,1:T(8,128)}, u32[]{:S(2)}) copy-start(f32[256,32]{0,1:T(8,128)} %param.14) | copy-start | bytes 98308
  944.2 295.9 %all-reduce.9.cloned.1.call-start = ((), (), s32[]{:S(2)}) async-start(), calls=%async_computation.6 | async-start | bytes 1048576 | tf_op jit(solution)/shard_map/psum | solution.py:44
  972.5 6.2 copy-start.1
  983.6 6.2 copy-start.1
  994.8 6.2 copy-start.1
  1005.9 6.2 copy-start.1
  1017.0 6.2 copy-start.1
  1028.1 6.2 copy-start.1
  1039.2 6.2 copy-start.1
  1050.3 6.2 copy-start.1
  1061.4 6.2 copy-start.1
  1072.6 6.2 copy-start.1
  1083.7 6.2 copy-start.1
  1094.8 6.2 copy-start.1
  1105.9 6.2 copy-start.1
  1117.0 6.2 copy-start.1
  1128.1 6.2 copy-start.1
  1139.2 6.2 copy-start.1
  1148.3 125.0 %copy-start.2 = (bf16[256,1024]{0,1:T(8,128)(2,1)S(1)}, bf16[256,1024]{0,1:T(8,128)(2,1)}, u32[]{:S(2)}) copy-start(bf16[256,1024]{0,1:T(8,128)(2,1)} %fusion.10) | copy-start | bytes 1572868
  1149.2 124.1 %all-reduce.11.cloned.1.call-start = ((), (), s32[]{:S(2)}) async-start(), calls=%async_computation.7 | async-start | bytes 131072 | tf_op jit(solution)/shard_map/psum | solution.py:49
  1251.7 61.6 %all-gather.11.cloned.1.call-start = ((), (), s32[]{:S(2)}) async-start(), calls=%async_computation.8 | async-start | bytes 1114112 | tf_op jit(solution)/shard_map/all_gather | solution.py:51
Sparse Core Ops, SparseCore 0:
  24.0 35.8 all-gather.4
  306.0 91.2 all-reduce.4
  409.1 21.3 all-reduce.6
  432.5 37.8 all-gather.6
  944.3 20.2 all-gather.8
  1149.3 90.6 all-reduce.8
  1251.8 21.3 all-reduce.10
  1275.5 37.8 all-gather.10
where the time goes:
time: 1800 us
  other arithmetic  770 us (43%)
  matrix products  496 us (28%)
  waiting for transfers between devices  423 us (24%)
  local copies, waits for them, and re-layouts  61 us (3%)
  loops' own time  23.5 us (1%)
    convert_element_type x96, other arithmetic, pair_cols(): table.reshape(val_block.shape[0] * cond_block.shape[0], width)  584 us
    dot_general x64, matrix products, decode_block(): lax.dot_general(pairs, coef_block, (((1,), (1,)), ((), ())), preferred_el...  379 us
    psum x2, waiting for transfers between devices, coupling(): summed = lax.psum(local_fit.astype(jnp.bfloat16), 'pts').astype(jnp.float32)  182 us
    convert_element_type x96, other arithmetic, pair_cols(): lax.dynamic_slice_in_dim(val_block, val_first, width, 1).astype(jnp.float32)  106 us
    dot_general x32, matrix products, local_block(): lax.dot_general(pairs, all_rows, (((0,), (0,)), ((), ())), preferred_elem...  93.5 us
    all_gather x2, waiting for transfers between devices, coupling(): field_piece = lax.all_gather(kernel_out, 'pts', axis=1, tiled=True)  78.5 us
    convert_element_type x96, other arithmetic, pair_cols(): lax.dynamic_slice_in_dim(cond_block, cond_first, width, 1)  74 us
    all_to_all x1, waiting for transfers between devices, on_device(): lax.all_to_all(orb_val, 'val', split_axis=1, concat_axis=0, tiled=True)  60.7 us
  transfers between devices with their start and end apart: 9, of which 9 were waited for; matrix products, arithmetic and copies ran while one was open for 0% of the time, Pallas kernels for 0%

commit v1 on v0

v1 whole, which is shorter than its diff:
```python
import math

import jax
import jax.numpy as jnp
from jax import lax
from jax.experimental import pallas as pl
from jax.experimental.pallas import tpu as pltpu
from jax.sharding import PartitionSpec as P

CENTER = 2.0
HALF_WIDTH = 1.5


def encode_kernel(rows_ref, val_ref, cond_ref, fit_ref):
    cond_count = cond_ref.shape[0]
    k = fit_ref.shape[0]
    total = jnp.zeros(fit_ref.shape, jnp.float32)
    half = jnp.dot(rows_ref[...], val_ref[...], preferred_element_type=jnp.float32)
    for c in range(cond_count):
        total += half[c * k:(c + 1) * k, :] * cond_ref[c:c + 1, :].astype(jnp.float32)
    fit_ref[...] = total.astype(fit_ref.dtype)


def encode(rows, orb_val, orb_cond, k):
    points = orb_val.shape[1]
    width = math.gcd(points, 512)
    return pl.pallas_call(
        encode_kernel,
        out_shape=jax.ShapeDtypeStruct((k, points), jnp.bfloat16),
        grid=(points // width,),
        in_specs=[
            pl.BlockSpec(rows.shape, lambda i: (0, 0)),
            pl.BlockSpec((orb_val.shape[0], width), lambda i: (0, i)),
            pl.BlockSpec((orb_cond.shape[0], width), lambda i: (0, i)),
        ],
        out_specs=pl.BlockSpec((k, width), lambda i: (0, i)),
        name="encode",
    )(rows, orb_val, orb_cond)


def decode_kernel(val_ref, cond_ref, field_ref, out_ref):
    @pl.when(pl.program_id(0) == 0)
    def _():
        out_ref[...] = jnp.zeros_like(out_ref)

    field = field_ref[...]
    spread = jnp.concatenate(
        [field * cond_ref[c:c + 1, :] for c in range(cond_ref.shape[0])], axis=0
    )
    out_ref[...] += lax.dot_general(
        spread, val_ref[...], (((1,), (1,)), ((), ())), preferred_element_type=jnp.float32
    )


def decode(orb_val, orb_cond, field):
    k, points = field.shape
    width = math.gcd(points, 1024)
    rows = orb_cond.shape[0] * k
    return pl.pallas_call(
        decode_kernel,
        out_shape=jax.ShapeDtypeStruct((rows, orb_val.shape[0]), jnp.float32),
        grid=(points // width,),
        in_specs=[
            pl.BlockSpec((orb_val.shape[0], width), lambda i: (0, i)),
            pl.BlockSpec((orb_cond.shape[0], width), lambda i: (0, i)),
            pl.BlockSpec((k, width), lambda i: (0, i)),
        ],
        out_specs=pl.BlockSpec((rows, orb_val.shape[0]), lambda i: (0, 0)),
        name="decode",
    )(orb_val, orb_cond, field)


def filter_apply(rows, gap_rows, orb_val, orb_cond, kernel, k):
    part = encode(rows, orb_val, orb_cond, k)
    own = lax.psum_scatter(part, "val", scatter_dimension=1, tiled=True)
    fit = lax.psum(own, "pts")
    kernel_part = lax.dot_general(
        fit, kernel, (((1,), (1,)), ((), ())), preferred_element_type=jnp.float32
    )
    piece = lax.psum(kernel_part.astype(jnp.bfloat16), "val")
    field = lax.all_gather(piece, "pts", axis=1, tiled=True)
    coupled = decode(orb_val, orb_cond, field)
    current = rows.astype(jnp.float32)
    return (gap_rows * current + 2.0 * coupled - CENTER * current) / HALF_WIDTH


def on_device(trial, energy_gap, orb_val, orb_cond, kernel):
    k = trial.shape[1] // orb_cond.shape[0]
    rows = trial.T
    gap_rows = jnp.repeat(energy_gap.T, k, axis=0)
    first = filter_apply(rows, gap_rows, orb_val, orb_cond, kernel, k).astype(jnp.bfloat16)
    second = 2.0 * filter_apply(first, gap_rows, orb_val, orb_cond, kernel, k)
    second = (second - rows.astype(jnp.float32)).astype(jnp.bfloat16)
    return first.T, second.T


def solution(mesh):
    placed = (P("val", "pts"), P("val", "pts"), P("val", None), P("pts", None), P("pts", "val"))
    return jax.shard_map(
        on_device,
        mesh=mesh,
        in_specs=placed,
        out_specs=(P("val", "pts"), P("val", "pts")),
        check_vma=False,
    )
```

time: 1800 us -> 483 us (0.27)
  other arithmetic: 770 us -> 3.83 us
  matrix products: 496 us -> 23.3 us
  Pallas kernels: 0 us -> 82.1 us
  waiting for transfers between devices: 423 us -> 353 us
  local copies, waits for them, and re-layouts: 61 us -> 4.06 us
  loops' own time: 23.5 us -> 0 us
    convert_element_type x290 -> x2, other arithmetic: 768 us -> 3.83 us  [the longest x1 2.28 us: on_device(): filter_apply(rows, gap_rows, orb_val, orb_cond, kernel, k)]
    dot_general x98 -> x2, matrix products: 496 us -> 23.3 us  [filter_apply(): lax.dot_general(fit, kernel, (((1,), (1,)), ((), ())), preferred_element_...]
    pallas_call x0 -> x4, Pallas kernels: none -> 82.1 us  [the longest x2 48.5 us: encode(): pl.pallas_call(encode_kernel, out_shape=jax.ShapeDtypeStruct((k, points),...]
    all_to_all x1 -> x0, waiting for transfers between devices: 60.7 us -> none  [on_device(): lax.all_to_all(orb_val, 'val', split_axis=1, concat_axis=0, tiled=True)]
    all_gather x4 -> x2, waiting for transfers between devices: 136 us -> 78.9 us  [filter_apply(): field = lax.all_gather(piece, 'pts', axis=1, tiled=True)]
    reduce_scatter x0 -> x2, waiting for transfers between devices: none -> 42.7 us  [filter_apply(): own = lax.psum_scatter(part, 'val', scatter_dimension=1, tiled=True)]
    another operation x4 -> x0, loops' own time: 23.5 us -> none  [the longest x2 21.1 us: coupling(): lax.map(local_block, jnp.arange(local_count, dtype=jnp.int32))]
    dynamic_slice x32 -> x0, local copies, waits for them, and re-layouts: 19.8 us -> none  [coupling(): lax.map(local_block, jnp.arange(local_count, dtype=jnp.int32))]
  transfers between devices with their start and end apart: 9 -> 8, of which waited for: 9 -> 8; matrix products, arithmetic and copies ran while one was open for 0% -> 0% of each run, Pallas kernels for 0% -> 0%
where the time goes in v1:
time: 483 us; the launch traced here: 481 us
  waiting for transfers between devices  353 us (73%)
  Pallas kernels  82.1 us (17%)
  matrix products  23.3 us (5%)
  between operations  14.2 us (3%)
    psum x2, waiting for transfers between devices, filter_apply(): fit = lax.psum(own, 'pts')  188 us
    all_gather x2, waiting for transfers between devices, filter_apply(): field = lax.all_gather(piece, 'pts', axis=1, tiled=True)  78.9 us
    pallas_call x2, Pallas kernels, encode(): pl.pallas_call(encode_kernel, out_shape=jax.ShapeDtypeStruct((k, points),...  48.5 us
    psum x2, waiting for transfers between devices, filter_apply(): piece = lax.psum(kernel_part.astype(jnp.bfloat16), 'val')  43 us
    reduce_scatter x2, waiting for transfers between devices, filter_apply(): own = lax.psum_scatter(part, 'val', scatter_dimension=1, tiled=True)  42.7 us
    pallas_call x2, Pallas kernels, decode(): pl.pallas_call(decode_kernel, out_shape=jax.ShapeDtypeStruct((rows, orb_v...  33.6 us
    dot_general x2, matrix products, filter_apply(): lax.dot_general(fit, kernel, (((1,), (1,)), ((), ())), preferred_element_...  23.3 us
  transfers between devices with their start and end apart: 8, of which 8 were waited for; matrix products, arithmetic and copies ran while one was open for 0% of the time, Pallas kernels for 0%

profile of v1, /device:TPU:0, one launch (start us, length us, event | category | flops | bytes accessed | tf_op | source)
XLA Modules:
  0.0 480.6 jit_solution(3776477163561037736)
XLA Ops:
  7.2 0.0 reduce-scatter.3.cloned.1.call-start
  7.2 2.0 copy.7
  9.3 24.3 %encode.2 = bf16[32,16384]{1,0:T(8,128)(2,1)} custom-call(bf16[1024,256]{1,0:T(8,128)(2,1)} %bitcast.21, bf16[256,16384]{1,0:T(8,128)(2,1)} %val_ref.7, bf16[32,16384]{1,0:T(8,128)(2,1)} %cond_ref.7), custom_call_target="tpu_custom_call" | custom-call | tf_op jit(solution)/shard_map/encode/pallas_call | solution.py:27
  33.5 0.0 copy-start
  33.5 0.0 copy-start.2
  33.5 0.0 reduce-scatter.3.cloned.1.call-update
  33.5 0.0 all-reduce.5.cloned.1.call-start
  33.6 23.2 %reduce-scatter.3.cloned.1.call-done = bf16[32,8192]{1,0:T(8,128)(2,1)} async-done(((bf16[32,16384]{1,0:T(8,128)(2,1)}), bf16[32,8192]{1,0:T(8,128)(2,1)}) %reduce-scatter.3.cloned.1.call-update) | async-done | bytes 524304 | tf_op jit(solution)/shard_map/reduce_scatter | solution.py:75
  56.8 0.0 all-reduce.5.cloned.1.call-update
  56.8 0.0 all-reduce.7.cloned.1.call-start
  56.9 94.1 %all-reduce.5.cloned.1.call-done = bf16[32,8192]{1,0:T(8,128)(2,1)} async-done(((bf16[32,8192]{1,0:T(8,128)(2,1)}), bf16[32,8192]{1,0:T(8,128)(2,1)}) %all-reduce.5.cloned.1.call-update) | async-done | bytes 524304 | tf_op jit(solution)/shard_map/psum | solution.py:76
  151.0 11.6 %convolution_convert_fusion.1 = bf16[32,1024]{1,0:T(8,128)(2,1)} fusion(bf16[32,8192]{1,0:T(8,128)(2,1)} %all-reduce.5.cloned.1.call-done, bf16[1024,8192]{1,0:T(8,128)(2,1)} %param.9), kind=kOutput, calls=%fused_computation.6 | convolution fusion | flops 536903680 | bytes 17367040 | tf_op jit(solution)/shard_map/dot_general | solution.py:77
  162.6 0.0 all-reduce.7.cloned.1.call-update
  162.6 0.0 all-gather.3.cloned.1.call-start
  162.7 21.5 %all-reduce.7.cloned.1.call-done = bf16[32,1024]{1,0:T(8,128)(2,1)} async-done(((bf16[32,1024]{1,0:T(8,128)(2,1)}), bf16[32,1024]{1,0:T(8,128)(2,1)}) %all-reduce.7.cloned.1.call-update) | async-done | bytes 65552 | tf_op jit(solution)/shard_map/psum | solution.py:80
  184.2 0.0 all-gather.3.cloned.1.call-update
  184.2 0.0 reduce-scatter.5.cloned.1.call-start
  184.3 39.9 %all-gather.3.cloned.1.call-done.field_ref = bf16[32,16384]{1,0:T(8,128)(2,1)} async-done(((bf16[32,1024]{1,0:T(8,128)(2,1)}), bf16[32,16384]{1,0:T(8,128)(2,1)}) %all-gather.3.cloned.1.call-update) | async-done | bytes 1048592 | tf_op jit(solution)/shard_map/all_gather | solution.py:81
  224.1 16.8 %decode.2 = f32[1024,256]{1,0:T(8,128)} custom-call(bf16[256,16384]{1,0:T(8,128)(2,1)} %val_ref.7, bf16[32,16384]{1,0:T(8,128)(2,1)} %cond_ref.7, bf16[32,16384]{1,0:T(8,128)(2,1)} %all-gather.3.cloned.1.call-done.field_ref), custom_call_target="tpu_custom_call" | custom-call | tf_op jit(solution)/shard_map/decode/pallas_call | solution.py:59
  240.9 0.0 copy-done
  240.9 0.0 copy-done.2
  240.9 2.3 fusion.4.rows_ref
  243.2 0.0 copy-start.1
  243.2 24.3 %encode.3 = bf16[32,16384]{1,0:T(8,128)(2,1)} custom-call(bf16[1024,256]{1,0:T(8,128)(2,1)} %fusion.4.rows_ref, bf16[256,16384]{1,0:T(8,128)(2,1)} %val_ref.7, bf16[32,16384]{1,0:T(8,128)(2,1)} %cond_ref.7), custom_call_target="tpu_custom_call" | custom-call | tf_op jit(solution)/shard_map/encode/pallas_call | solution.py:27
  267.5 0.0 reduce-scatter.5.cloned.1.call-update
  267.5 0.0 all-reduce.9.cloned.1.call-start
  267.6 19.5 %reduce-scatter.5.cloned.1.call-done = bf16[32,8192]{1,0:T(8,128)(2,1)} async-done(((bf16[32,16384]{1,0:T(8,128)(2,1)}), bf16[32,8192]{1,0:T(8,128)(2,1)}) %reduce-scatter.5.cloned.1.call-update) | async-done | bytes 524304 | tf_op jit(solution)/shard_map/reduce_scatter | solution.py:75
  287.1 0.0 all-reduce.9.cloned.1.call-update
  287.1 0.0 all-reduce.11.cloned.1.call-start
  287.1 93.9 %all-reduce.9.cloned.1.call-done = bf16[32,8192]{1,0:T(8,128)(2,1)} async-done(((bf16[32,8192]{1,0:T(8,128)(2,1)}), bf16[32,8192]{1,0:T(8,128)(2,1)}) %all-reduce.9.cloned.1.call-update) | async-done | bytes 524304 | tf_op jit(solution)/shard_map/psum | solution.py:76
  381.1 11.6 %convolution_convert_fusion = bf16[32,1024]{1,0:T(8,128)(2,1)} fusion(bf16[32,8192]{1,0:T(8,128)(2,1)} %all-reduce.9.cloned.1.call-done, bf16[1024,8192]{1,0:T(8,128)(2,1)} %param.9), kind=kOutput, calls=%fused_computation.5 | convolution fusion | flops 536903680 | bytes 17367040 | tf_op jit(solution)/shard_map/dot_general | solution.py:77
  392.7 0.0 all-reduce.11.cloned.1.call-update
  392.8 0.0 all-gather.5.cloned.1.call-start
  392.8 21.5 %all-reduce.11.cloned.1.call-done = bf16[32,1024]{1,0:T(8,128)(2,1)} async-done(((bf16[32,1024]{1,0:T(8,128)(2,1)}), bf16[32,1024]{1,0:T(8,128)(2,1)}) %all-reduce.11.cloned.1.call-update) | async-done | bytes 65552 | tf_op jit(solution)/shard_map/psum | solution.py:80
  414.3 0.0 all-gather.5.cloned.1.call-update
  414.3 0.0 copy-done.1
  414.3 1.0 copy.8
  415.4 39.0 %all-gather.5.cloned.1.call-done.field_ref = bf16[32,16384]{1,0:T(8,128)(2,1)} async-done(((bf16[32,1024]{1,0:T(8,128)(2,1)}), bf16[32,16384]{1,0:T(8,128)(2,1)}) %all-gather.5.cloned.1.call-update) | async-done | bytes 1048592 | tf_op jit(solution)/shard_map/all_gather | solution.py:81
  454.4 16.8 %decode.3 = f32[1024,256]{1,0:T(8,128)} custom-call(bf16[256,16384]{1,0:T(8,128)(2,1)} %val_ref.7, bf16[32,16384]{1,0:T(8,128)(2,1)} %cond_ref.7, bf16[32,16384]{1,0:T(8,128)(2,1)} %all-gather.5.cloned.1.call-done.field_ref), custom_call_target="tpu_custom_call" | custom-call | tf_op jit(solution)/shard_map/decode/pallas_call | solution.py:59
  471.2 1.5 fusion.5
  472.7 1.0 copy.9
Async XLA Ops:
  7.2 49.6 %reduce-scatter.3.cloned.1.call-start = ((), (), s32[]{:S(2)}) async-start(), calls=%async_computation.2 | async-start | bytes 1572864 | tf_op jit(solution)/shard_map/reduce_scatter | solution.py:75
  33.5 207.4 %copy-start = (bf16[256,1024]{0,1:T(8,128)(2,1)S(1)}, bf16[256,1024]{0,1:T(8,128)(2,1)}, u32[]{:S(2)}) copy-start(bf16[256,1024]{0,1:T(8,128)(2,1)} %copy.7) | copy-start | bytes 1572868
  33.5 207.4 %copy-start.2 = (f32[256,32]{0,1:T(8,128)S(1)}, f32[256,32]{0,1:T(8,128)}, u32[]{:S(2)}) copy-start(f32[256,32]{0,1:T(8,128)} %param.6) | copy-start | bytes 98308
  33.5 117.4 %all-reduce.5.cloned.1.call-start = ((), (), s32[]{:S(2)}) async-start(), calls=%async_computation.3 | async-start | bytes 1048576 | tf_op jit(solution)/shard_map/psum | solution.py:76
  56.8 127.4 %all-reduce.7.cloned.1.call-start = ((), (), s32[]{:S(2)}) async-start(), calls=%async_computation.4 | async-start | bytes 131072 | tf_op jit(solution)/shard_map/psum | solution.py:80
  162.6 61.5 %all-gather.3.cloned.1.call-start = ((), (), s32[]{:S(2)}) async-start(), calls=%async_computation.5 | async-start | bytes 1114112 | tf_op jit(solution)/shard_map/all_gather | solution.py:81
  184.2 102.9 %reduce-scatter.5.cloned.1.call-start = ((), (), s32[]{:S(2)}) async-start(), calls=%async_computation.6 | async-start | bytes 1572864 | tf_op jit(solution)/shard_map/reduce_scatter | solution.py:75
  243.2 171.1 %copy-start.1 = (bf16[1024,256]{1,0:T(8,128)(2,1)S(1)}, bf16[1024,256]{1,0:T(8,128)(2,1)}, u32[]{:S(2)}) copy-start(bf16[1024,256]{1,0:T(8,128)(2,1)} %fusion.4.rows_ref) | copy-start | bytes 1572868
  267.5 113.6 %all-reduce.9.cloned.1.call-start = ((), (), s32[]{:S(2)}) async-start(), calls=%async_computation.7 | async-start | bytes 1048576 | tf_op jit(solution)/shard_map/psum | solution.py:76
  287.1 127.2 %all-reduce.11.cloned.1.call-start = ((), (), s32[]{:S(2)}) async-start(), calls=%async_computation.8 | async-start | bytes 131072 | tf_op jit(solution)/shard_map/psum | solution.py:80
  392.8 61.6 %all-gather.5.cloned.1.call-start = ((), (), s32[]{:S(2)}) async-start(), calls=%async_computation.9 | async-start | bytes 1114112 | tf_op jit(solution)/shard_map/all_gather | solution.py:81
Sparse Core Ops, SparseCore 0:
  33.7 23.0 reduce-scatter.2
  60.2 90.7 all-reduce.4
  162.8 21.3 all-reduce.6
  186.2 37.8 all-gather.2
  267.6 19.3 reduce-scatter.4
  290.3 90.7 all-reduce.8
  392.9 21.3 all-reduce.10
  416.5 37.8 all-gather.4

commit v2 on v1

--- a/solution.py
+++ b/solution.py
@@ -1,3 +1,4 @@
+import functools
 import math
 
 import jax
@@ -9,6 +10,203 @@
 
 CENTER = 2.0
 HALF_WIDTH = 1.5
+MESH = pl.DeviceIdType.MESH
+F32 = jnp.float32
+BF16 = jnp.bfloat16
+
+
+def filter_kernel(sizes, rows_ref, gap_ref, cond_ref, val_hbm, kern_hbm, first_ref, second_ref,
+                  val_ref, kern_ref, source, total, product, away, home, got_core, mixed, got_val, mid,
+                  got_y, low, got_z, fit, part, got_part, field,
+                  val_sem, kern_sem, send_sem, recv_sem):
+    A, Y, Z = sizes
+    Q = Y * Z
+    B = 2 * Q
+    k, w = fit.shape[-2:]
+    R = field.shape[-1]
+    cond_count = cond_ref.shape[0]
+    a = lax.axis_index("val")
+    p = lax.axis_index("pts")
+    h = lax.rem(p, 2)
+    y = lax.rem(p // 2, Y)
+    z = p // (2 * Y)
+
+    def around(base, shift, size):
+        return lax.rem(base + shift + size, size)
+
+    def at(val, zz, yy, hh):
+        return (val, (zz * Y + yy) * 2 + hh)
+
+    other = at(a, z, y, 1 - h)
+    vals = [at(around(a, d, A), z, y, h) for d in range(1, A)]
+    ys = [at(a, z, around(y, d, Y), h) for d in range(1, Y)]
+    zs = [at(a, around(z, d, Z), y, h) for d in range(1, Z)]
+
+    def val_copy(i):
+        cols = pl.ds(pl.multiple_of(i * w, w), w)
+        return pltpu.make_async_copy(val_hbm.at[:, cols], val_ref.at[:, cols], val_sem.at[i])
+
+    def piece_number(val, half, j):
+        return (val * 2 + half) * Q + j
+
+    def fetch(val, half):
+        @pl.loop(0, Q)
+        def _(j):
+            val_copy(piece_number(val, half, j)).start()
+
+    order = [around(a, d, A) for d in range(1, A)] + [a]
+    for half in (1 - h, h):
+        for b in order:
+            fetch(b, half)
+    kern_copy = pltpu.make_async_copy(kern_hbm, kern_ref, kern_sem)
+    kern_copy.start()
+
+    barrier = pltpu.get_barrier_semaphore()
+    peers = [other] + vals + ys + zs
+    for peer in peers:
+        pl.semaphore_signal(barrier, inc=1, device_id=peer, device_id_type=MESH)
+    pl.semaphore_wait(barrier, len(peers))
+
+    source[...] = rows_ref[...]
+
+    @pl.loop(0, 2)
+    def _(step):
+        number = [0]
+        started = []
+
+        def send(src, dst, peer):
+            slot = number[0]
+            number[0] += 1
+            copy = pltpu.make_async_remote_copy(
+                src_ref=src, dst_ref=dst, send_sem=send_sem.at[step, slot],
+                recv_sem=recv_sem.at[step, slot], device_id=peer, device_id_type=MESH)
+            copy.start()
+            started.append(copy)
+            return copy
+
+        def encode(val, half, target, slot):
+            @pl.loop(0, Q)
+            def _(j):
+                i = piece_number(val, half, j)
+
+                @pl.when(step == 0)
+                def _():
+                    val_copy(i).wait()
+
+                cols = pl.ds(pl.multiple_of(i * w, w), w)
+                full = jnp.dot(source[...], val_ref[:, cols], preferred_element_type=F32)
+                cond = cond_ref[:, cols].astype(F32)
+                summed = jnp.zeros((k, w), F32)
+                for c in range(cond_count):
+                    summed += full[c * k:(c + 1) * k, :] * cond[c:c + 1, :]
+                target[slot, j] = summed.astype(BF16)
+
+        core_copies = []
+        for n, b in enumerate(order):
+            encode(b, 1 - h, away.at[step], n)
+            core_copies.append(send(away.at[step, n], got_core.at[step, n], other))
+        val_copies = []
+        for n, b in enumerate(order):
+            encode(b, h, home.at[step], n)
+            core_copies[n].wait_recv()
+            mixed[step, n] = (home[step, n].astype(F32) + got_core[step, n].astype(F32)).astype(BF16)
+            if n < A - 1:
+                val_copies.append(send(mixed.at[step, n], got_val.at[step, n], vals[n]))
+        summed = mixed[step, A - 1].astype(F32)
+        for n, copy in enumerate(val_copies):
+            copy.wait_recv()
+            summed += got_val[step, n].astype(F32)
+        mid[step] = summed.astype(BF16).reshape(mid.shape[1:])
+        copies = [send(mid.at[step, around(y, n + 1, Y)], got_y.at[step, n], peer)
+                  for n, peer in enumerate(ys)]
+        summed = mid[step, y].astype(F32)
+        for n, copy in enumerate(copies):
+            copy.wait_recv()
+            summed += got_y[step, n].astype(F32)
+        low[step] = summed.astype(BF16)
+        copies = [send(low.at[step, around(z, n + 1, Z)], got_z.at[step, n], peer)
+                  for n, peer in enumerate(zs)]
+        summed = low[step, z].astype(F32)
+        for n, copy in enumerate(copies):
+            copy.wait_recv()
+            summed += got_z[step, n].astype(F32)
+        fit[step, h, y, z] = summed.astype(BF16)
+
+        def gather(buffer, use):
+            mine = buffer.at[step, h, y, z]
+            z_copies = [send(mine, mine, peer) for peer in zs]
+            y_copies = {}
+            core_copies = []
+
+            def spread(dz):
+                zz = around(z, -dz, Z)
+                ref = buffer.at[step, h, y, zz]
+                for n, peer in enumerate(ys):
+                    y_copies[(n, dz)] = send(ref, ref, peer)
+                core_copies.append((send(ref, ref, other), y, zz))
+                use(h, y, zz)
+
+            spread(0)
+            for dz in range(1, Z):
+                z_copies[dz - 1].wait_recv()
+                spread(dz)
+            for n in range(Y - 1):
+                yy = around(y, -(n + 1), Y)
+                for dz in range(Z):
+                    zz = around(z, -dz, Z)
+                    y_copies[(n, dz)].wait_recv()
+                    ref = buffer.at[step, h, yy, zz]
+                    core_copies.append((send(ref, ref, other), yy, zz))
+                    use(h, yy, zz)
+            for copy, yy, zz in core_copies:
+                copy.wait_recv()
+                use(1 - h, yy, zz)
+
+        product[...] = jnp.zeros_like(product)
+
+        @pl.when(step == 0)
+        def _():
+            kern_copy.wait()
+
+        def apply_kernel(hh, yy, zz):
+            cols = pl.ds(pl.multiple_of(((hh * Y + yy) * Z + zz) * w, w), w)
+            product[...] += lax.dot_general(
+                kern_ref[:, cols], fit[step, hh, yy, zz], (((1,), (1,)), ((), ())),
+                preferred_element_type=F32)
+
+        gather(fit, apply_kernel)
+        part[step] = product[...].T.astype(BF16)
+        copies = [send(part.at[step], got_part.at[step, n], peer) for n, peer in enumerate(vals)]
+        summed = part[step].astype(F32)
+        for n, copy in enumerate(copies):
+            copy.wait_recv()
+            summed += got_part[step, n].astype(F32)
+        field[step, h, y, z] = summed.astype(BF16)
+
+        total[...] = jnp.zeros_like(total)
+
+        def decode(hh, yy, zz):
+            cols = pl.ds(pl.multiple_of(((zz * Y + yy) * 2 + hh) * R, R), R)
+            piece = field[step, hh, yy, zz]
+            cond = cond_ref[:, cols]
+            table = jnp.concatenate([piece * cond[c:c + 1, :] for c in range(cond_count)], axis=0)
+            total[...] += lax.dot_general(
+                table, val_ref[:, cols], (((1,), (1,)), ((), ())), preferred_element_type=F32)
+
+        gather(field, decode)
+        current = source[...].astype(F32)
+        applied = (gap_ref[...] * current + 2.0 * total[...] - CENTER * current) / HALF_WIDTH
+
+        @pl.when(step == 0)
+        def _():
+            source[...] = applied.astype(BF16)
+            first_ref[...] = applied.astype(BF16)
+
+        @pl.when(step == 1)
+        def _():
+            second_ref[...] = (2.0 * applied - rows_ref[...].astype(F32)).astype(BF16)
+        for copy in started:
+            copy.wait_send()
 
 
 def encode_kernel(rows_ref, val_ref, cond_ref, fit_ref):
@@ -70,7 +268,7 @@
     )(orb_val, orb_cond, field)
 
 
-def filter_apply(rows, gap_rows, orb_val, orb_cond, kernel, k):
+def staged_apply(rows, gap_rows, orb_val, orb_cond, kernel, k):
     part = encode(rows, orb_val, orb_cond, k)
     own = lax.psum_scatter(part, "val", scatter_dimension=1, tiled=True)
     fit = lax.psum(own, "pts")
@@ -84,20 +282,64 @@
     return (gap_rows * current + 2.0 * coupled - CENTER * current) / HALF_WIDTH
 
 
-def on_device(trial, energy_gap, orb_val, orb_cond, kernel):
+def on_device(A, B, trial, energy_gap, orb_val, orb_cond, kernel):
     k = trial.shape[1] // orb_cond.shape[0]
     rows = trial.T
     gap_rows = jnp.repeat(energy_gap.T, k, axis=0)
-    first = filter_apply(rows, gap_rows, orb_val, orb_cond, kernel, k).astype(jnp.bfloat16)
-    second = 2.0 * filter_apply(first, gap_rows, orb_val, orb_cond, kernel, k)
-    second = (second - rows.astype(jnp.float32)).astype(jnp.bfloat16)
+    Q = B // 2
+    Z = math.gcd(Q, 4)
+    Y = Q // Z
+    points = orb_val.shape[1]
+    w = points // (A * B)
+    R = points // B
+    if w % 128:
+        first = staged_apply(rows, gap_rows, orb_val, orb_cond, kernel, k).astype(BF16)
+        second = 2.0 * staged_apply(first, gap_rows, orb_val, orb_cond, kernel, k)
+        return first.T, (second - rows.astype(F32)).astype(BF16).T
+    sends = A + (A - 1) * 2 + (Y - 1) + (Z - 1) + 2 * (Z - 1 + (Y - 1) * Z + Q)
+    vmem = pl.BlockSpec(memory_space=pltpu.VMEM)
+    anywhere = pl.BlockSpec(memory_space=pl.ANY)
+    shape = jax.ShapeDtypeStruct(rows.shape, BF16)
+    first, second = pl.pallas_call(
+        functools.partial(filter_kernel, (A, Y, Z)),
+        out_shape=(shape, shape),
+        in_specs=[vmem, vmem, vmem, anywhere, anywhere],
+        out_specs=(vmem, vmem),
+        scratch_shapes=[
+            pltpu.VMEM(orb_val.shape, BF16),
+            pltpu.VMEM(kernel.shape, BF16),
+            pltpu.VMEM(rows.shape, BF16),
+            pltpu.VMEM(rows.shape, F32),
+            pltpu.VMEM((R, k), F32),
+            pltpu.VMEM((2, A, Q, k, w), BF16),
+            pltpu.VMEM((2, A, Q, k, w), BF16),
+            pltpu.VMEM((2, A, Q, k, w), BF16),
+            pltpu.VMEM((2, A, Q, k, w), BF16),
+            pltpu.VMEM((2, max(A - 1, 1), Q, k, w), BF16),
+            pltpu.VMEM((2, Y, Z, k, w), BF16),
+            pltpu.VMEM((2, max(Y - 1, 1), Z, k, w), BF16),
+            pltpu.VMEM((2, Z, k, w), BF16),
+            pltpu.VMEM((2, max(Z - 1, 1), k, w), BF16),
+            pltpu.VMEM((2, 2, Y, Z, k, w), BF16),
+            pltpu.VMEM((2, k, R), BF16),
+            pltpu.VMEM((2, max(A - 1, 1), k, R), BF16),
+            pltpu.VMEM((2, 2, Y, Z, k, R), BF16),
+            pltpu.SemaphoreType.DMA((A * B,)),
+            pltpu.SemaphoreType.DMA,
+            pltpu.SemaphoreType.DMA((2, sends)),
+            pltpu.SemaphoreType.DMA((2, sends)),
+        ],
+        compiler_params=pltpu.CompilerParams(
+            collective_id=0, has_side_effects=True, vmem_limit_bytes=60 << 20),
+        name="filter",
+    )(rows, gap_rows, orb_cond, orb_val, kernel)
     return first.T, second.T
 
 
 def solution(mesh):
     placed = (P("val", "pts"), P("val", "pts"), P("val", None), P("pts", None), P("pts", "val"))
     return jax.shard_map(
-        on_device,
+        functools.partial(on_device, mesh.shape["val"], mesh.shape["pts"]),
         mesh=mesh,
         in_specs=placed,
         out_specs=(P("val", "pts"), P("val", "pts")),

time: 483 us -> 146 us (0.30)
  waiting for transfers between devices: 353 us -> 0 us
  Pallas kernels: 82.1 us -> 137 us
  matrix products: 23.3 us -> 0 us
  between operations: 14.2 us -> 0.64 us
    psum x4 -> x0, waiting for transfers between devices: 231 us -> none  [the longest x2 188 us: filter_apply(): fit = lax.psum(own, 'pts')]
    all_gather x2 -> x0, waiting for transfers between devices: 78.9 us -> none  [filter_apply(): field = lax.all_gather(piece, 'pts', axis=1, tiled=True)]
    pallas_call x4 -> x1, Pallas kernels: 82.1 us -> 137 us  [on_device(): pl.pallas_call(functools.partial(filter_kernel, (A, Y, Z)), out_shape=(sh...]
    reduce_scatter x2 -> x0, waiting for transfers between devices: 42.7 us -> none  [filter_apply(): own = lax.psum_scatter(part, 'val', scatter_dimension=1, tiled=True)]
    dot_general x2 -> x0, matrix products: 23.3 us -> none  [filter_apply(): lax.dot_general(fit, kernel, (((1,), (1,)), ((), ())), preferred_element_...]
  transfers between devices with their start and end apart: 8 -> 0, of which waited for: 8 -> 0; matrix products, arithmetic and copies ran while one was open for 0% -> 0% of each run, Pallas kernels for 0% -> 0%
where the time goes in v2:
time: 146 us
  Pallas kernels  137 us (94%)
  local copies, waits for them, and re-layouts  7.95 us (5%)
    pallas_call x1, Pallas kernels, on_device(): pl.pallas_call(functools.partial(filter_kernel, (A, Y, Z)), out_shape=(sh...  137 us
    unnamed x3, local copies, waits for them, and re-layouts  6.12 us

profile of v2, /device:TPU:0, one launch (start us, length us, event | category | flops | bytes accessed | tf_op | source)
XLA Modules:
  0.0 146.0 jit_solution(11951803999928297128)
XLA Ops:
  0.6 2.0 %copy.7 = bf16[256,1024]{0,1:T(8,128)(2,1)} copy(bf16[256,1024]{1,0:T(8,128)(2,1)} %param.5) | data formatting | bytes 1048576 | tf_op args[0]
  2.7 1.8 %broadcast_in_dim.3 = f32[32,32,256]{2,1,0:T(8,128)} broadcast(f32[32,256]{1,0:T(8,128)} %bitcast.9), dimensions={0,2} | broadcast | bytes 1081344 | tf_op jit(solution)/shard_map/broadcast_in_dim | solution.py:288
  4.5 137.4 %filter.1 = (bf16[1024,256]{1,0:T(8,128)(2,1)}, bf16[1024,256]{1,0:T(8,128)(2,1)}) custom-call(bf16[1024,256]{1,0:T(8,128)(2,1)} %bitcast.6, f32[1024,256]{1,0:T(8,128)} %bitcast.5, bf16[32,16384]{1,0:T(8,128)(2,1)} %cond_ref.1, bf16[256,16384]{1,0:T(8,128)(2,1)} %val_hbm.1, bf16[1024,8192]{1,0:T(8,128)(2,1)} %kern_hbm.1), custom_call_target="tpu_custom_call" | custom-call | tf_op jit(solution)/shard_map/filter/pallas_call | solution.py:303
  141.9 2.0 %copy.8 = bf16[256,1024]{1,0:T(8,128)(2,1)} copy(bf16[256,1024]{0,1:T(8,128)(2,1)} %bitcast.8) | data formatting | bytes 1048576
  144.0 2.0 %copy.9 = bf16[256,1024]{1,0:T(8,128)(2,1)} copy(bf16[256,1024]{0,1:T(8,128)(2,1)} %bitcast.7) | data formatting | bytes 1048576

commit v3 on v2

--- a/solution.py
+++ b/solution.py
@@ -69,17 +69,17 @@
 
     source[...] = rows_ref[...]
 
-    @pl.loop(0, 2)
-    def _(step):
+    def chain(step, i):
         number = [0]
         started = []
+        rows = pl.ds(i * cond_count * k, cond_count * k)
 
         def send(src, dst, peer):
             slot = number[0]
             number[0] += 1
             copy = pltpu.make_async_remote_copy(
-                src_ref=src, dst_ref=dst, send_sem=send_sem.at[step, slot],
-                recv_sem=recv_sem.at[step, slot], device_id=peer, device_id_type=MESH)
+                src_ref=src, dst_ref=dst, send_sem=send_sem.at[step, i, slot],
+                recv_sem=recv_sem.at[step, i, slot], device_id=peer, device_id_type=MESH)
             copy.start()
             started.append(copy)
             return copy
@@ -87,14 +87,14 @@
         def encode(val, half, target, slot):
             @pl.loop(0, Q)
             def _(j):
-                i = piece_number(val, half, j)
-
-                @pl.when(step == 0)
-                def _():
-                    val_copy(i).wait()
-
-                cols = pl.ds(pl.multiple_of(i * w, w), w)
-                full = jnp.dot(source[...], val_ref[:, cols], preferred_element_type=F32)
+                n = piece_number(val, half, j)
+                if i == 0:
+                    @pl.when(step == 0)
+                    def _():
+                        val_copy(n).wait()
+
+                cols = pl.ds(pl.multiple_of(n * w, w), w)
+                full = jnp.dot(source[rows, :], val_ref[:, cols], preferred_element_type=F32)
                 cond = cond_ref[:, cols].astype(F32)
                 summed = jnp.zeros((k, w), F32)
                 for c in range(cond_count):
@@ -103,110 +103,132 @@
 
         core_copies = []
         for n, b in enumerate(order):
-            encode(b, 1 - h, away.at[step], n)
-            core_copies.append(send(away.at[step, n], got_core.at[step, n], other))
+            encode(b, 1 - h, away.at[step, i], n)
+            core_copies.append(send(away.at[step, i, n], got_core.at[step, i, n], other))
+            yield
         val_copies = []
         for n, b in enumerate(order):
-            encode(b, h, home.at[step], n)
+            encode(b, h, home.at[step, i], n)
             core_copies[n].wait_recv()
-            mixed[step, n] = (home[step, n].astype(F32) + got_core[step, n].astype(F32)).astype(BF16)
+            mixed[step, i, n] = (home[step, i, n].astype(F32)
+                                 + got_core[step, i, n].astype(F32)).astype(BF16)
             if n < A - 1:
-                val_copies.append(send(mixed.at[step, n], got_val.at[step, n], vals[n]))
-        summed = mixed[step, A - 1].astype(F32)
+                val_copies.append(send(mixed.at[step, i, n], got_val.at[step, i, n], vals[n]))
+            yield
+        summed = mixed[step, i, A - 1].astype(F32)
         for n, copy in enumerate(val_copies):
             copy.wait_recv()
-            summed += got_val[step, n].astype(F32)
-        mid[step] = summed.astype(BF16).reshape(mid.shape[1:])
-        copies = [send(mid.at[step, around(y, n + 1, Y)], got_y.at[step, n], peer)
+            summed += got_val[step, i, n].astype(F32)
+        mid[step, i] = summed.astype(BF16).reshape(mid.shape[2:])
+        copies = [send(mid.at[step, i, around(y, n + 1, Y)], got_y.at[step, i, n], peer)
                   for n, peer in enumerate(ys)]
-        summed = mid[step, y].astype(F32)
+        yield
+        summed = mid[step, i, y].astype(F32)
         for n, copy in enumerate(copies):
             copy.wait_recv()
-            summed += got_y[step, n].astype(F32)
-        low[step] = summed.astype(BF16)
-        copies = [send(low.at[step, around(z, n + 1, Z)], got_z.at[step, n], peer)
+            summed += got_y[step, i, n].astype(F32)
+        low[step, i] = summed.astype(BF16)
+        copies = [send(low.at[step, i, around(z, n + 1, Z)], got_z.at[step, i, n], peer)
                   for n, peer in enumerate(zs)]
-        summed = low[step, z].astype(F32)
+        yield
+        summed = low[step, i, z].astype(F32)
         for n, copy in enumerate(copies):
             copy.wait_recv()
-            summed += got_z[step, n].astype(F32)
-        fit[step, h, y, z] = summed.astype(BF16)
+            summed += got_z[step, i, n].astype(F32)
+        fit[step, i, h, y, z] = summed.astype(BF16)
 
         def gather(buffer, use):
-            mine = buffer.at[step, h, y, z]
+            mine = buffer.at[step, i, h, y, z]
             z_copies = [send(mine, mine, peer) for peer in zs]
             y_copies = {}
             core_copies = []
 
             def spread(dz):
                 zz = around(z, -dz, Z)
-                ref = buffer.at[step, h, y, zz]
+                ref = buffer.at[step, i, h, y, zz]
                 for n, peer in enumerate(ys):
                     y_copies[(n, dz)] = send(ref, ref, peer)
                 core_copies.append((send(ref, ref, other), y, zz))
                 use(h, y, zz)
 
             spread(0)
+            yield
             for dz in range(1, Z):
                 z_copies[dz - 1].wait_recv()
                 spread(dz)
+                yield
             for n in range(Y - 1):
                 yy = around(y, -(n + 1), Y)
                 for dz in range(Z):
                     zz = around(z, -dz, Z)
                     y_copies[(n, dz)].wait_recv()
-                    ref = buffer.at[step, h, yy, zz]
+                    ref = buffer.at[step, i, h, yy, zz]
                     core_copies.append((send(ref, ref, other), yy, zz))
                     use(h, yy, zz)
-            for copy, yy, zz in core_copies:
+                    if dz % 2:
+                        yield
+            for n, (copy, yy, zz) in enumerate(core_copies):
                 copy.wait_recv()
                 use(1 - h, yy, zz)
-
-        product[...] = jnp.zeros_like(product)
+                if n % 2:
+                    yield
+
+        product[i] = jnp.zeros(product.shape[1:], F32)
+        if i == 0:
+            @pl.when(step == 0)
+            def _():
+                kern_copy.wait()
+
+        def apply_kernel(hh, yy, zz):
+            cols = pl.ds(pl.multiple_of(((hh * Y + yy) * Z + zz) * w, w), w)
+            product[i] += lax.dot_general(
+                kern_ref[:, cols], fit[step, i, hh, yy, zz], (((1,), (1,)), ((), ())),
+                preferred_element_type=F32)
+
+        yield from gather(fit, apply_kernel)
+        part[step, i] = product[i].T.astype(BF16)
+        copies = [send(part.at[step, i], got_part.at[step, i, n], peer)
+                  for n, peer in enumerate(vals)]
+        yield
+        summed = part[step, i].astype(F32)
+        for n, copy in enumerate(copies):
+            copy.wait_recv()
+            summed += got_part[step, i, n].astype(F32)
+        field[step, i, h, y, z] = summed.astype(BF16)
+
+        total[rows, :] = jnp.zeros((cond_count * k, total.shape[1]), F32)
+
+        def decode(hh, yy, zz):
+            cols = pl.ds(pl.multiple_of(((zz * Y + yy) * 2 + hh) * R, R), R)
+            piece = field[step, i, hh, yy, zz]
+            cond = cond_ref[:, cols]
+            table = jnp.concatenate([piece * cond[c:c + 1, :] for c in range(cond_count)], axis=0)
+            total[rows, :] += lax.dot_general(
+                table, val_ref[:, cols], (((1,), (1,)), ((), ())), preferred_element_type=F32)
+
+        yield from gather(field, decode)
+        current = source[rows, :].astype(F32)
+        applied = (gap_ref[...] * current + 2.0 * total[rows, :] - CENTER * current) / HALF_WIDTH
 
         @pl.when(step == 0)
         def _():
-            kern_copy.wait()
-
-        def apply_kernel(hh, yy, zz):
-            cols = pl.ds(pl.multiple_of(((hh * Y + yy) * Z + zz) * w, w), w)
-            product[...] += lax.dot_general(
-                kern_ref[:, cols], fit[step, hh, yy, zz], (((1,), (1,)), ((), ())),
-                preferred_element_type=F32)
-
-        gather(fit, apply_kernel)
-        part[step] = product[...].T.astype(BF16)
-        copies = [send(part.at[step], got_part.at[step, n], peer) for n, peer in enumerate(vals)]
-        summed = part[step].astype(F32)
-        for n, copy in enumerate(copies):
-            copy.wait_recv()
-            summed += got_part[step, n].astype(F32)
-        field[step, h, y, z] = summed.astype(BF16)
-
-        total[...] = jnp.zeros_like(total)
-
-        def decode(hh, yy, zz):
-            cols = pl.ds(pl.multiple_of(((zz * Y + yy) * 2 + hh) * R, R), R)
-            piece = field[step, hh, yy, zz]
-            cond = cond_ref[:, cols]
-            table = jnp.concatenate([piece * cond[c:c + 1, :] for c in range(cond_count)], axis=0)
-            total[...] += lax.dot_general(
-                table, val_ref[:, cols], (((1,), (1,)), ((), ())), preferred_element_type=F32)
-
-        gather(field, decode)
-        current = source[...].astype(F32)
-        applied = (gap_ref[...] * current + 2.0 * total[...] - CENTER * current) / HALF_WIDTH
-
-        @pl.when(step == 0)
-        def _():
-            source[...] = applied.astype(BF16)
-            first_ref[...] = applied.astype(BF16)
+            source[rows, :] = applied.astype(BF16)
+            first_ref[rows, :] = applied.astype(BF16)
 
         @pl.when(step == 1)
         def _():
-            second_ref[...] = (2.0 * applied - rows_ref[...].astype(F32)).astype(BF16)
+            second_ref[rows, :] = (2.0 * applied - rows_ref[rows, :].astype(F32)).astype(BF16)
+
         for copy in started:
             copy.wait_send()
+
+    @pl.loop(0, 2)
+    def _(step):
+        live = [chain(step, 0), chain(step, 1)]
+        for _ in range(2 * A - 1):
+            next(live[0])
+        while live:
+            live = [part_chain for part_chain in live if next(part_chain, True) is None]
 
 
 def encode_kernel(rows_ref, val_ref, cond_ref, fit_ref):
@@ -299,6 +321,10 @@
     sends = A + (A - 1) * 2 + (Y - 1) + (Z - 1) + 2 * (Z - 1 + (Y - 1) * Z + Q)
     vmem = pl.BlockSpec(memory_space=pltpu.VMEM)
     anywhere = pl.BlockSpec(memory_space=pl.ANY)
+    cond_count = orb_cond.shape[0]
+    kk = k // 2
+    rows = trial.reshape(-1, cond_count, 2, kk).transpose(2, 1, 3, 0).reshape(rows.shape)
+    gap_rows = jnp.repeat(energy_gap.T, kk, axis=0)
     shape = jax.ShapeDtypeStruct(rows.shape, BF16)
     first, second = pl.pallas_call(
         functools.partial(filter_kernel, (A, Y, Z)),
@@ -310,30 +336,35 @@
             pltpu.VMEM(kernel.shape, BF16),
             pltpu.VMEM(rows.shape, BF16),
             pltpu.VMEM(rows.shape, F32),
-            pltpu.VMEM((R, k), F32),
-            pltpu.VMEM((2, A, Q, k, w), BF16),
-            pltpu.VMEM((2, A, Q, k, w), BF16),
-            pltpu.VMEM((2, A, Q, k, w), BF16),
-            pltpu.VMEM((2, A, Q, k, w), BF16),
-            pltpu.VMEM((2, max(A - 1, 1), Q, k, w), BF16),
-            pltpu.VMEM((2, Y, Z, k, w), BF16),
-            pltpu.VMEM((2, max(Y - 1, 1), Z, k, w), BF16),
-            pltpu.VMEM((2, Z, k, w), BF16),
-            pltpu.VMEM((2, max(Z - 1, 1), k, w), BF16),
-            pltpu.VMEM((2, 2, Y, Z, k, w), BF16),
-            pltpu.VMEM((2, k, R), BF16),
-            pltpu.VMEM((2, max(A - 1, 1), k, R), BF16),
-            pltpu.VMEM((2, 2, Y, Z, k, R), BF16),
+            pltpu.VMEM((2, R, kk), F32),
+            pltpu.VMEM((2, 2, A, Q, kk, w), BF16),
+            pltpu.VMEM((2, 2, A, Q, kk, w), BF16),
+            pltpu.VMEM((2, 2, A, Q, kk, w), BF16),
+            pltpu.VMEM((2, 2, A, Q, kk, w), BF16),
+            pltpu.VMEM((2, 2, max(A - 1, 1), Q, kk, w), BF16),
+            pltpu.VMEM((2, 2, Y, Z, kk, w), BF16),
+            pltpu.VMEM((2, 2, max(Y - 1, 1), Z, kk, w), BF16),
+            pltpu.VMEM((2, 2, Z, kk, w), BF16),
+            pltpu.VMEM((2, 2, max(Z - 1, 1), kk, w), BF16),
+            pltpu.VMEM((2, 2, 2, Y, Z, kk, w), BF16),
+            pltpu.VMEM((2, 2, kk, R), BF16),
+            pltpu.VMEM((2, 2, max(A - 1, 1), kk, R), BF16),
+            pltpu.VMEM((2, 2, 2, Y, Z, kk, R), BF16),
             pltpu.SemaphoreType.DMA((A * B,)),
             pltpu.SemaphoreType.DMA,
-            pltpu.SemaphoreType.DMA((2, sends)),
-            pltpu.SemaphoreType.DMA((2, sends)),
+            pltpu.SemaphoreType.DMA((2, 2, sends)),
+            pltpu.SemaphoreType.DMA((2, 2, sends)),
         ],
         compiler_params=pltpu.CompilerParams(
             collective_id=0, has_side_effects=True, vmem_limit_bytes=60 << 20),
         name="filter",
     )(rows, gap_rows, orb_cond, orb_val, kernel)
-    return first.T, second.T
+
+    def back(out):
+        out = out.reshape(2, cond_count, kk, -1).transpose(3, 1, 0, 2)
+        return out.reshape(trial.shape)
+
+    return back(first), back(second)
 
 
 def solution(mesh):

time: 146 us -> 163 us (1.12)
  Pallas kernels: 137 us -> 154 us
    pallas_call x1, Pallas kernels: 137 us -> 154 us  [on_device(): pl.pallas_call(functools.partial(filter_kernel, (A, Y, Z)), out_shape=(sh...]
    unnamed x3, local copies, waits for them, and re-layouts: 6.12 us -> 3.26 us
    reshape x0 -> x2, local copies, waits for them, and re-layouts: none -> 2.2 us  [back(): out = out.reshape(2, cond_count, kk, -1).transpose(3, 1, 0, 2)]
where the time goes in v3:
time: 163 us; the launch traced here: 162 us
  Pallas kernels  154 us (94%)
  local copies, waits for them, and re-layouts  7.88 us (5%)
    pallas_call x1, Pallas kernels, on_device(): pl.pallas_call(functools.partial(filter_kernel, (A, Y, Z)), out_shape=(sh...  154 us

profile of v3, /device:TPU:0, one launch (start us, length us, event | category | flops | bytes accessed | tf_op | source)
XLA Modules:
  0.0 162.4 jit_solution(4945480514170216173)
XLA Ops:
  0.6 1.2 copy.10
  1.9 0.8 copy.11
  2.7 1.6 broadcast_in_dim.3
  4.3 153.9 %filter.1 = (bf16[1024,256]{1,0:T(8,128)(2,1)}, bf16[1024,256]{1,0:T(8,128)(2,1)}) custom-call(bf16[1024,256]{1,0:T(8,128)(2,1)} %bitcast.17, f32[512,256]{1,0:T(8,128)} %bitcast.18, bf16[32,16384]{1,0:T(8,128)(2,1)} %cond_ref.1, bf16[256,16384]{1,0:T(8,128)(2,1)} %val_hbm.1, bf16[1024,8192]{1,0:T(8,128)(2,1)} %kern_hbm.1), custom_call_target="tpu_custom_call" | custom-call | tf_op jit(solution)/shard_map/filter/pallas_call | solution.py:329
  158.2 1.1 copy.12
  159.3 1.0 copy.14
  160.3 1.1 copy.13
  161.4 1.0 copy.15
